TPU v7x, 256 devices: a whole 4x4x8 slice. The times are simulated.
256 devices in a mesh: ep: 32 (over x, z), tp: 8 (over y, core).
Axes of the slice: x: 4, y: 4, z: 8, core: 2. Of those that a mesh axis runs over, the one named last changes fastest.
Arguments:
- attn_out: bfloat16 [8192, 2048], P('ep', 'tp'), may hold values from -6 to 6
- out_proj: bfloat16 [2048, 2048], P('tp'), may hold values from -0.125 to 0.125
- residual: bfloat16 [8192, 2048], P('ep'), may hold values from -40 to 40
- norm_gain: float32 [2048], replicated, may hold values from 0.25 to 1.75
- router: bfloat16 [2048, 64], replicated, may hold values from -0.125 to 0.125
- expert_gate_up: bfloat16 [256, 2, 352, 2048], P(('ep', 'tp')), may hold values from -0.125 to 0.125
- expert_down: bfloat16 [256, 352, 2048], P(('ep', 'tp')), may hold values from -0.15625 to 0.15625
- shared_gate_up: bfloat16 [2, 2816, 2048], P(None, 'tp'), may hold values from -0.125 to 0.125
- shared_down: bfloat16 [2816, 2048], P('tp'), may hold values from -0.109375 to 0.109375
- routes: int32 [8192, 6], P('ep'), may hold values from 0 to 63, all different within a row; in each aligned block of 256 rows (0 to 255, 256 to 511, ...) at most 40 rows name the same one
- live_rows: int32 [32], P('ep'), may hold values from 128 to 256, as said below
- next_gain: float32 [2048], replicated, may hold values from 0.25 to 1.75
Outputs:
- next_stream: bfloat16 [8192, 2048], P('ep', 'tp')
- next_normed: bfloat16 [8192, 2048], P('ep', 'tp')
Inputs may be any that keep to these rules, and one draw needn't show every extreme that they name: `routes`: each row names 6 different experts. Among the 256 rows of one block no expert is named by more than 40 rows, a bound that some block reaches. The live rows of block b are its first live_rows[b] rows; in every draw some block is entirely live.
All inputs are finite; a program needn't handle non-finite values.
Results may differ from a plain program's by a relative error of at most 0.012.
Values may be sent and summed in bfloat16 or wider, within the bound.
A program may use at most 128 MiB of HBM per device.

v0:
```python
import jax
import jax.numpy as jnp
from jax import lax
from jax.sharding import PartitionSpec as P

EXP_DEV = 2
norm_epsilon = 1e-06
routed_scale = 2.446


def slot_table(route_block, live_count, experts, capacity):
    fanout = route_block.shape[1]
    flat_ids = route_block.reshape(-1)
    entry_index = jnp.arange(flat_ids.shape[0], dtype=jnp.int32)
    living = entry_index // fanout < live_count
    one_hot = (
        (flat_ids[:, None] == jnp.arange(experts, dtype=jnp.int32)[None, :]) & living[:, None]
    ).astype(jnp.int32)
    earlier = jnp.cumsum(one_hot, axis=0, dtype=jnp.int32) - one_hot
    position = jnp.sum(earlier * one_hot, axis=1, dtype=jnp.int32)
    slot_index = jnp.where(living, flat_ids * capacity + position, experts * capacity)
    slot_owner = (
        jnp.full((experts * capacity,), -1, jnp.int32).at[slot_index].set(entry_index, mode="drop")
    )
    return (slot_index, living, slot_owner)


def gate_weights(normed, router, route_block):
    logits = jnp.dot(normed, router, preferred_element_type=jnp.float32)
    chosen = jnp.take_along_axis(logits, route_block, axis=1)
    scores = jax.nn.sigmoid(chosen)
    return scores / jnp.sum(scores, axis=1, keepdims=True) * routed_scale


def on_device(
    attn_out,
    out_proj,
    residual,
    norm_gain,
    router,
    expert_gate_up,
    expert_down,
    shared_gate_up,
    shared_down,
    routes,
    live_rows,
    next_gain,
):
    partial_out = jnp.dot(attn_out, out_proj, preferred_element_type=jnp.float32)
    summed = lax.psum(partial_out, "tp")
    stream = (summed + residual.astype(jnp.float32)).astype(jnp.bfloat16)
    stream_wide = stream.astype(jnp.float32)
    normed = (
        stream_wide
        * lax.rsqrt(jnp.mean(stream_wide * stream_wide, axis=1, keepdims=True) + norm_epsilon)
        * norm_gain
    ).astype(jnp.bfloat16)
    width = normed.shape[1]
    tp_count = lax.axis_size("tp")
    ep_count = lax.axis_size("ep")
    width_slice = width // tp_count
    column_start = lax.axis_index("tp") * width_slice
    unit_blocks = tp_count // EXP_DEV
    group = lax.axis_index("tp") // unit_blocks
    experts = router.shape[1]
    fanout = routes.shape[1]
    token_rows = routes.shape[0]
    capacity = token_rows * fanout * 5 // (3 * experts)
    slot_index, living, slot_owner = slot_table(routes, live_rows[0], experts, capacity)
    owners = slot_owner.reshape(ep_count, EXP_DEV, capacity)
    filled = owners >= 0
    source_row = jnp.where(filled, owners // fanout, 0)
    dispatched = jnp.where(filled[:, :, :, None], normed[source_row], jnp.zeros((), jnp.bfloat16))
    rows = lax.dynamic_index_in_dim(
        lax.all_to_all(dispatched, "ep", split_axis=0, concat_axis=0, tiled=True),
        group,
        1,
        keepdims=False,
    )
    gate_proj = jnp.einsum(
        "scd,fd->scf", rows, expert_gate_up[0, 0], preferred_element_type=jnp.float32
    )
    up_proj = jnp.einsum(
        "scd,fd->scf", rows, expert_gate_up[0, 1], preferred_element_type=jnp.float32
    )
    hidden = (jax.nn.silu(gate_proj) * up_proj).astype(jnp.bfloat16)
    produced = jnp.einsum(
        "scf,fd->scd", hidden, expert_down[0], preferred_element_type=jnp.float32
    ).astype(jnp.bfloat16)
    returned = lax.all_to_all(produced, "ep", split_axis=0, concat_axis=0, tiled=True)
    flat_terms = returned.reshape(ep_count * capacity, width)
    living_pairs = living.reshape(token_rows, fanout)
    mine = living_pairs & (routes % EXP_DEV == group)
    position = slot_index.reshape(token_rows, fanout) - routes * capacity
    term_row = jnp.where(mine, routes // EXP_DEV * capacity + position, 0)
    weights = gate_weights(normed, router, routes) * mine.astype(jnp.float32)
    picked = flat_terms[term_row]
    routed_part = jnp.einsum("tkd,tk->td", picked.astype(jnp.float32), weights)
    shared_gate = jnp.einsum(
        "td,fd->tf", normed, shared_gate_up[0], preferred_element_type=jnp.float32
    )
    shared_up = jnp.einsum(
        "td,fd->tf", normed, shared_gate_up[1], preferred_element_type=jnp.float32
    )
    shared_hidden = (jax.nn.silu(shared_gate) * shared_up).astype(jnp.bfloat16)
    shared_part = jnp.dot(shared_hidden, shared_down, preferred_element_type=jnp.float32)
    combined = lax.psum_scatter(
        (routed_part + shared_part).astype(jnp.bfloat16), "tp", scatter_dimension=1, tiled=True
    ).astype(jnp.float32)
    stream_slice = lax.dynamic_slice_in_dim(stream, column_start, width_slice, 1)
    next_stream = (stream_slice.astype(jnp.float32) + combined).astype(jnp.bfloat16)
    next_wide = next_stream.astype(jnp.float32)
    squares = lax.psum(jnp.sum(next_wide * next_wide, axis=1), "tp")
    gain_slice = lax.dynamic_slice_in_dim(next_gain, column_start, width_slice, 0)
    next_normed = (
        next_wide * lax.rsqrt(squares[:, None] / width + norm_epsilon) * gain_slice
    ).astype(jnp.bfloat16)
    return (next_stream, next_normed)


def solution(mesh):
    in_specs = (
        P("ep", "tp"),
        P("tp", None),
        P("ep", None),
        P(),
        P(),
        P(("ep", "tp"), None, None, None),
        P(("ep", "tp"), None, None),
        P(None, "tp", None),
        P("tp", None),
        P("ep", None),
        P("ep"),
        P(),
    )
    out_specs = (P("ep", "tp"), P("ep", "tp"))
    return jax.shard_map(
        on_device, mesh=mesh, in_specs=in_specs, out_specs=out_specs, check_vma=False
    )
```

profile of v0, /device:TPU:1, one launch (start us, length us, event | category | flops | bytes accessed | tf_op | source)
XLA Modules:
  0.0 608.2 jit_solution(8504731297024068242)
XLA Ops:
  7.2 3.1 fusion.76
  11.6 18.1 %reduce-window.6 = s32[64,12,128]{2,1,0:T(8,128)S(1)} reduce-window(s32[64,12,128]{2,1,0:T(8,128)S(1)} %fusion.37, s32[]{:T(128)} %constant.103.clone.1), window={size=1x1x128 pad=0_0x0_0x127_0}, to_apply=%region_1.0 | reduce-window | flops 12484608 | bytes 786436 | tf_op jit(solution)/shard_map/reduce-window
  29.7 0.2 slice.30
  29.9 0.3 copy.44
  30.3 0.2 broadcast_add_fusion
  31.3 6.2 %scatter_custom_fusion = s32[2560]{0:T(1024)S(1)} fusion(s32[1536]{0:T(1024)S(1)} %fusion.67, s32[1536]{0:T(1024)S(1)} %iota.72, s32[]{:T(128)} %constant.107.clone.1), kind=kCustom, calls=%fused_computation.112 | custom fusion | bytes 10244 | tf_op jit(solution)/shard_map/scatter | solution.py:23
  37.7 0.7 ge.27
  38.8 0.6 pad_clamp_fusion
  39.4 44.1 %all-reduce.2.cloned.1.call-done = f32[256,2048]{1,0:T(8,128)} async-done(((f32[256,2048]{1,0:T(8,128)}), f32[256,2048]{1,0:T(8,128)}) %all-reduce.2.cloned.1.call-update) | async-done | bytes 2097168 | tf_op jit(solution)/shard_map/psum | solution.py:50
  83.4 2.3 fusion.7
  85.7 0.3 fusion.9
  86.0 10.9 %gather_fusion = bf16[2560,2048]{1,0:T(8,128)(2,1)} fusion(bf16[256,2048]{1,0:T(8,128)(2,1)S(1)} %fusion.9, s32[3072]{0:T(1024)} %pad_clamp_fusion), kind=kCustom, calls=%fused_computation | custom fusion | bytes 20981760 | tf_op jit(solution)/shard_map/gather | solution.py:73
  97.0 10.0 %broadcast_select_fusion = bf16[32,2,40,2048]{3,2,1,0:T(8,128)(2,1)} fusion(bf16[32,2,40,2048]{3,2,1,0:T(8,128)(2,1)} %bitcast.83, pred[32,2,40]{2,1,0:T(4,128)(4,1)} %ge.27), kind=kLoop, calls=%fused_computation.4 | loop fusion | flops 5242880 | bytes 20974080 | tf_op jit(solution)/shard_map/jit(_where)/select_n | solution.py:73
  106.9 9.7 %all-to-all-start = ((bf16[32,2,40,2048]{3,2,1,0:T(8,128)(2,1)}), bf16[32,2,40,2048]{3,2,1,0:T(8,128)(2,1)}, u32[]{:S(2)}, u32[]{:S(2)}) async-start(bf16[32,2,40,2048]{3,2,1,0:T(8,128)(2,1)} %broadcast_select_fusion), calls=%async_computation | async-start | bytes 20971520 | tf_op jit(solution)/shard_map/all_to_all | solution.py:75
  116.6 232.0 %all-to-all-done = bf16[32,2,40,2048]{3,2,1,0:T(8,128)(2,1)} async-done(((bf16[32,2,40,2048]{3,2,1,0:T(8,128)(2,1)}), bf16[32,2,40,2048]{3,2,1,0:T(8,128)(2,1)}, u32[]{:S(2)}, u32[]{:S(2)}) %all-to-all-start) | async-done | bytes 10485792 | tf_op jit(solution)/shard_map/all_to_all | solution.py:75
  348.6 7.1 %fusion.2 = f32[32,40,352]{2,1,0:T(8,128)} fusion(bf16[32,2,40,2048]{3,2,1,0:T(8,128)(2,1)} %all-to-all-done, s32[]{:T(128)S(6)} %select_n.135, bf16[1,2,352,2048]{3,2,1,0:T(8,128)(2,1)} %param.17), kind=kOutput, calls=%fused_computation.7 | convolution fusion | flops 1845493760 | bytes 8486916 | tf_op jit(solution)/shard_map/scd,fd->scf/dot_general | solution.py:80
  355.7 9.8 %convolution_convert_fusion = bf16[32,40,2048]{2,1,0:T(8,128)(2,1)} fusion(bf16[1,352,2048]{2,1,0:T(8,128)(2,1)S(1)} %copy-done, f32[32,40,352]{2,1,0:T(8,128)} %fusion.2, bf16[32,2,40,2048]{3,2,1,0:T(8,128)(2,1)} %all-to-all-done, s32[]{:T(128)S(6)} %select_n.135, bf16[1,2,352,2048]{3,2,1,0:T(8,128)(2,1)} %param.17), kind=kOutput, calls=%fused_computation.11 | convolution fusion | flops 3696312320 | bytes 15335428 | tf_op jit(solution)/shard_map/scf,fd->scd/dot_general | solution.py:87
  365.5 10.2 %all-to-all-start.1 = ((bf16[32,40,2048]{2,1,0:T(8,128)(2,1)}), bf16[32,40,2048]{2,1,0:T(8,128)(2,1)}, u32[]{:S(2)}, u32[]{:S(2)}) async-start(bf16[32,40,2048]{2,1,0:T(8,128)(2,1)} %convolution_convert_fusion), calls=%async_computation.1 | async-start | bytes 10485760 | tf_op jit(solution)/shard_map/all_to_all | solution.py:90
  375.7 0.2 reduce-scatter.2.cloned.1.call-start
  376.6 0.4 fusion.77
  377.0 12.7 %gather_fusion.2 = f32[1536]{0:T(1024)S(1)} fusion(f32[256,64]{0,1:T(8,128)S(1)} %fusion.77, s32[1536]{0:T(1024)S(1)} %reshape.237), kind=kCustom, calls=%fused_computation.2 | custom fusion | bytes 24576 | tf_op jit(solution)/shard_map/jit(take_along_axis)/gather | solution.py:30
  390.2 2.7 fusion.16
  392.9 99.9 %all-to-all-done.1 = bf16[32,40,2048]{2,1,0:T(8,128)(2,1)} async-done(((bf16[32,40,2048]{2,1,0:T(8,128)(2,1)}), bf16[32,40,2048]{2,1,0:T(8,128)(2,1)}, u32[]{:S(2)}, u32[]{:S(2)}) %all-to-all-start.1) | async-done | bytes 5242912 | tf_op jit(solution)/shard_map/all_to_all | solution.py:90
  492.8 15.8 %gather_fusion.1 = bf16[1536,2048]{1,0:T(8,128)(2,1)} fusion(bf16[1280,2048]{1,0:T(8,128)(2,1)} %bitcast.11, s32[2048]{0:T(1024)S(1)} %pad_clamp_fusion.1), kind=kCustom, calls=%fused_computation.1 | custom fusion | bytes 12589056 | tf_op jit(solution)/shard_map/gather | solution.py:97
  508.7 10.9 %reshape.230 = bf16[256,6,2048]{2,1,0:T(8,128)(2,1)} reshape(bf16[1536,2048]{1,0:T(8,128)(2,1)} %gather_fusion.1) | data formatting | bytes 12582912 | tf_op jit(solution)/shard_map/gather | solution.py:97
  519.6 7.1 %fusion.78 = f32[256,1,2048]{2,1,0:T(1,128)} fusion(bf16[256,6,2048]{2,1,0:T(8,128)(2,1)} %reshape.230, bf16[256,6,1]{1,2,0:T(2,128)(2,1)S(1)} %copy.50), kind=kOutput, calls=%fused_computation.124 | convolution fusion | flops 6291456 | bytes 8391680 | tf_op jit(solution)/shard_map/tkd,tk->td/dot_general | solution.py:98
  526.7 5.9 fusion.6
  532.6 0.8 dynamic_slice.12
  533.4 51.3 %reduce-scatter.2.cloned.1.call-done = bf16[256,256]{1,0:T(8,128)(2,1)} async-done(((bf16[256,2048]{1,0:T(8,128)(2,1)}), bf16[256,256]{1,0:T(8,128)(2,1)}) %reduce-scatter.2.cloned.1.call-update) | async-done | bytes 131088 | tf_op jit(solution)/shard_map/reduce_scatter | solution.py:107
  584.7 1.0 fusion.47
  585.7 14.9 %psum.15 = f32[256]{0:T(256)S(1)} all-reduce(f32[256]{0:T(256)S(1)} %get-tuple-element.2), channel_id=1, replica_groups=mesh['ep'=32,'tp'=8] {'tp'}, use_global_device_ids=true, to_apply=%region_9.10 | all-reduce | flops 256 | bytes 2048 | tf_op jit(solution)/shard_map/psum | solution.py:113
  600.6 0.8 fusion.49
  (51 shorter events, 3.0 us)
Async XLA Ops:
  7.2 348.5 %copy-start = (bf16[1,352,2048]{2,1,0:T(8,128)(2,1)S(1)}, bf16[1,352,2048]{2,1,0:T(8,128)(2,1)}, u32[]{:S(2)}) copy-start(bf16[1,352,2048]{2,1,0:T(8,128)(2,1)} %param.18) | copy-start | bytes 4325380
  7.2 3.2 copy-start.4
  7.2 76.2 %all-reduce.2.cloned.1.call-start = ((), (), s32[]{:S(2)}) async-start(), calls=%async_computation.3 | async-start | bytes 4194304 | tf_op jit(solution)/shard_map/psum | solution.py:50
  83.4 2.3 copy-start.5
  106.9 241.7 %all-to-all-start = ((bf16[32,2,40,2048]{3,2,1,0:T(8,128)(2,1)}), bf16[32,2,40,2048]{3,2,1,0:T(8,128)(2,1)}, u32[]{:S(2)}, u32[]{:S(2)}) async-start(bf16[32,2,40,2048]{3,2,1,0:T(8,128)(2,1)} %broadcast_select_fusion), calls=%async_computation | async-start | bytes 20971520 | tf_op jit(solution)/shard_map/all_to_all | solution.py:75
  365.5 11.1 %copy-start.3 = (bf16[2048,64]{0,1:T(8,128)(2,1)S(1)}, bf16[2048,64]{0,1:T(8,128)(2,1)}, u32[]{:S(2)}) copy-start(bf16[2048,64]{0,1:T(8,128)(2,1)} %param.16) | copy-start | bytes 786436
  365.5 127.3 %all-to-all-start.1 = ((bf16[32,40,2048]{2,1,0:T(8,128)(2,1)}), bf16[32,40,2048]{2,1,0:T(8,128)(2,1)}, u32[]{:S(2)}, u32[]{:S(2)}) async-start(bf16[32,40,2048]{2,1,0:T(8,128)(2,1)} %convolution_convert_fusion), calls=%async_computation.1 | async-start | bytes 10485760 | tf_op jit(solution)/shard_map/all_to_all | solution.py:90
  375.7 209.0 %reduce-scatter.2.cloned.1.call-start = ((), (), s32[]{:S(2)}) async-start(), calls=%async_computation.4 | async-start | bytes 1179648 | tf_op jit(solution)/shard_map/reduce_scatter | solution.py:107
  526.7 74.7 %copy-start.1 = (bf16[1,352,2048]{2,1,0:T(8,128)(2,1)S(1)}, bf16[1,352,2048]{2,1,0:T(8,128)(2,1)}, u32[]{:S(2)}) copy-start(bf16[1,352,2048]{2,1,0:T(8,128)(2,1)} %param.18) | copy-start | bytes 4325380
  585.7 15.7 %copy-start.2 = (bf16[256,256]{1,0:T(8,128)(2,1)}, bf16[256,256]{1,0:T(8,128)(2,1)S(1)}, u32[]{:S(2)}) copy-start(bf16[256,256]{1,0:T(8,128)(2,1)S(1)} %get-tuple-element.3) | copy-start | bytes 393220
Sparse Core Ops, SparseCore 0:
  10.5 72.8 all-reduce.1
  532.7 51.9 reduce-scatter.1
where the time goes:
time: 609 us; the launch traced here: 608 us
  waiting for transfers between devices  427 us (70%)
  local copies, waits for them, and re-layouts  60.9 us (10%)
  matrix products  36.1 us (6%)
  other arithmetic  33.8 us (6%)
  starting transfers between devices  20.1 us (3%)
  between operations  15 us (2%)
  blocking collectives  14.9 us (2%)
    all_to_all x1, waiting for transfers between devices, on_device(): lax.all_to_all(dispatched, 'ep', split_axis=0, concat_axis=0, tiled=True)  232 us
    all_to_all x1, waiting for transfers between devices, on_device(): lax.all_to_all(produced, 'ep', split_axis=0, concat_axis=0, tiled=True)  99.9 us
    reduce_scatter x1, waiting for transfers between devices, on_device(): lax.psum_scatter((routed_part + shared_part).astype(jnp.bfloat16), 'tp',...  51.3 us
    psum x1, waiting for transfers between devices, on_device(): summed = lax.psum(partial_out, 'tp')  44.1 us
    gather x2, local copies, waits for them, and re-layouts, on_device(): picked = flat_terms[term_row]  26.8 us
    another operation x3, other arithmetic  18.4 us
    psum x1, blocking collectives, on_device(): squares = lax.psum(jnp.sum(next_wide * next_wide, axis=1), 'tp')  14.9 us
    gather x5, local copies, waits for them, and re-layouts, gate_weights(): chosen = jnp.take_along_axis(logits, route_block, axis=1)  13.2 us
  transfers between devices with their start and end apart: 4, of which 4 were waited for; matrix products, arithmetic and copies ran while one was open for 8% of the time, Pallas kernels for 0%

commit v1 on v0

--- a/solution.py
+++ b/solution.py
@@ -110,7 +110,7 @@
     stream_slice = lax.dynamic_slice_in_dim(stream, column_start, width_slice, 1)
     next_stream = (stream_slice.astype(jnp.float32) + combined).astype(jnp.bfloat16)
     next_wide = next_stream.astype(jnp.float32)
-    squares = lax.psum(jnp.sum(next_wide * next_wide, axis=1), "tp")
+    squares = jnp.sum(lax.all_gather(jnp.sum(next_wide * next_wide, axis=1), "tp"), axis=0)
     gain_slice = lax.dynamic_slice_in_dim(next_gain, column_start, width_slice, 0)
     next_normed = (
         next_wide * lax.rsqrt(squares[:, None] / width + norm_epsilon) * gain_slice

time: 609 us -> 605 us (level)
    psum x1 -> x0, blocking collectives: 14.9 us -> none  [on_device(): squares = lax.psum(jnp.sum(next_wide * next_wide, axis=1), 'tp')]
    all_gather x0 -> x1, blocking collectives: none -> 10.7 us  [on_device(): lax.all_gather(jnp.sum(next_wide * next_wide, axis=1), 'tp')]
where the time goes in v1:
time: 605 us; the launch traced here: 604 us
  waiting for transfers between devices  427 us (71%)
  local copies, waits for them, and re-layouts  60.9 us (10%)
  matrix products  36.1 us (6%)
  other arithmetic  33.9 us (6%)
  starting transfers between devices  20.1 us (3%)
  between operations  15 us (2%)
  blocking collectives  10.7 us (2%)
    all_to_all x1, waiting for transfers between devices, on_device(): lax.all_to_all(dispatched, 'ep', split_axis=0, concat_axis=0, tiled=True)  232 us
    all_to_all x1, waiting for transfers between devices, on_device(): lax.all_to_all(produced, 'ep', split_axis=0, concat_axis=0, tiled=True)  99.9 us
    reduce_scatter x1, waiting for transfers between devices, on_device(): lax.psum_scatter((routed_part + shared_part).astype(jnp.bfloat16), 'tp',...  51.3 us
    psum x1, waiting for transfers between devices, on_device(): summed = lax.psum(partial_out, 'tp')  44.1 us
    gather x2, local copies, waits for them, and re-layouts, on_device(): picked = flat_terms[term_row]  26.8 us
    another operation x3, other arithmetic  18.4 us
    gather x5, local copies, waits for them, and re-layouts, gate_weights(): chosen = jnp.take_along_axis(logits, route_block, axis=1)  13.2 us
  transfers between devices with their start and end apart: 4, of which 4 were waited for; matrix products, arithmetic and copies ran while one was open for 8% of the time, Pallas kernels for 0%

profile of v1, /device:TPU:1, one launch (start us, length us, event | category | flops | bytes accessed | tf_op | source)
XLA Modules:
  0.0 604.1 jit_solution(5712165033433359267)
XLA Ops:
  7.2 3.1 fusion.76
  11.6 18.1 %reduce-window.6 = s32[64,12,128]{2,1,0:T(8,128)S(1)} reduce-window(s32[64,12,128]{2,1,0:T(8,128)S(1)} %fusion.37, s32[]{:T(128)} %constant.103.clone.1), window={size=1x1x128 pad=0_0x0_0x127_0}, to_apply=%region_1.0 | reduce-window | flops 12484608 | bytes 786436 | tf_op jit(solution)/shard_map/reduce-window
  29.7 0.2 slice.30
  29.9 0.3 copy.44
  30.3 0.2 broadcast_add_fusion
  31.3 6.2 %scatter_custom_fusion = s32[2560]{0:T(1024)S(1)} fusion(s32[1536]{0:T(1024)S(1)} %fusion.67, s32[1536]{0:T(1024)S(1)} %iota.72, s32[]{:T(128)} %constant.107.clone.1), kind=kCustom, calls=%fused_computation.112 | custom fusion | bytes 10244 | tf_op jit(solution)/shard_map/scatter | solution.py:23
  37.7 0.7 ge.27
  38.8 0.6 pad_clamp_fusion
  39.4 44.1 %all-reduce.2.cloned.1.call-done = f32[256,2048]{1,0:T(8,128)} async-done(((f32[256,2048]{1,0:T(8,128)}), f32[256,2048]{1,0:T(8,128)}) %all-reduce.2.cloned.1.call-update) | async-done | bytes 2097168 | tf_op jit(solution)/shard_map/psum | solution.py:50
  83.4 2.3 fusion.7
  85.7 0.3 fusion.9
  86.0 10.9 %gather_fusion = bf16[2560,2048]{1,0:T(8,128)(2,1)} fusion(bf16[256,2048]{1,0:T(8,128)(2,1)S(1)} %fusion.9, s32[3072]{0:T(1024)} %pad_clamp_fusion), kind=kCustom, calls=%fused_computation | custom fusion | bytes 20981760 | tf_op jit(solution)/shard_map/gather | solution.py:73
  97.0 10.0 %broadcast_select_fusion = bf16[32,2,40,2048]{3,2,1,0:T(8,128)(2,1)} fusion(bf16[32,2,40,2048]{3,2,1,0:T(8,128)(2,1)} %bitcast.84, pred[32,2,40]{2,1,0:T(4,128)(4,1)} %ge.27), kind=kLoop, calls=%fused_computation.4 | loop fusion | flops 5242880 | bytes 20974080 | tf_op jit(solution)/shard_map/jit(_where)/select_n | solution.py:73
  106.9 9.7 %all-to-all-start = ((bf16[32,2,40,2048]{3,2,1,0:T(8,128)(2,1)}), bf16[32,2,40,2048]{3,2,1,0:T(8,128)(2,1)}, u32[]{:S(2)}, u32[]{:S(2)}) async-start(bf16[32,2,40,2048]{3,2,1,0:T(8,128)(2,1)} %broadcast_select_fusion), calls=%async_computation | async-start | bytes 20971520 | tf_op jit(solution)/shard_map/all_to_all | solution.py:75
  116.6 232.0 %all-to-all-done = bf16[32,2,40,2048]{3,2,1,0:T(8,128)(2,1)} async-done(((bf16[32,2,40,2048]{3,2,1,0:T(8,128)(2,1)}), bf16[32,2,40,2048]{3,2,1,0:T(8,128)(2,1)}, u32[]{:S(2)}, u32[]{:S(2)}) %all-to-all-start) | async-done | bytes 10485792 | tf_op jit(solution)/shard_map/all_to_all | solution.py:75
  348.6 7.1 %fusion.2 = f32[32,40,352]{2,1,0:T(8,128)} fusion(bf16[32,2,40,2048]{3,2,1,0:T(8,128)(2,1)} %all-to-all-done, s32[]{:T(128)S(6)} %select_n.135, bf16[1,2,352,2048]{3,2,1,0:T(8,128)(2,1)} %param.17), kind=kOutput, calls=%fused_computation.7 | convolution fusion | flops 1845493760 | bytes 8486916 | tf_op jit(solution)/shard_map/scd,fd->scf/dot_general | solution.py:80
  355.7 9.8 %convolution_convert_fusion = bf16[32,40,2048]{2,1,0:T(8,128)(2,1)} fusion(bf16[1,352,2048]{2,1,0:T(8,128)(2,1)S(1)} %copy-done, f32[32,40,352]{2,1,0:T(8,128)} %fusion.2, bf16[32,2,40,2048]{3,2,1,0:T(8,128)(2,1)} %all-to-all-done, s32[]{:T(128)S(6)} %select_n.135, bf16[1,2,352,2048]{3,2,1,0:T(8,128)(2,1)} %param.17), kind=kOutput, calls=%fused_computation.11 | convolution fusion | flops 3696312320 | bytes 15335428 | tf_op jit(solution)/shard_map/scf,fd->scd/dot_general | solution.py:87
  365.5 10.2 %all-to-all-start.1 = ((bf16[32,40,2048]{2,1,0:T(8,128)(2,1)}), bf16[32,40,2048]{2,1,0:T(8,128)(2,1)}, u32[]{:S(2)}, u32[]{:S(2)}) async-start(bf16[32,40,2048]{2,1,0:T(8,128)(2,1)} %convolution_convert_fusion), calls=%async_computation.1 | async-start | bytes 10485760 | tf_op jit(solution)/shard_map/all_to_all | solution.py:90
  375.7 0.2 reduce-scatter.2.cloned.1.call-start
  376.6 0.4 fusion.77
  377.0 12.7 %gather_fusion.2 = f32[1536]{0:T(1024)S(1)} fusion(f32[256,64]{0,1:T(8,128)S(1)} %fusion.77, s32[1536]{0:T(1024)S(1)} %reshape.241), kind=kCustom, calls=%fused_computation.2 | custom fusion | bytes 24576 | tf_op jit(solution)/shard_map/jit(take_along_axis)/gather | solution.py:30
  390.2 2.7 fusion.16
  392.9 99.9 %all-to-all-done.1 = bf16[32,40,2048]{2,1,0:T(8,128)(2,1)} async-done(((bf16[32,40,2048]{2,1,0:T(8,128)(2,1)}), bf16[32,40,2048]{2,1,0:T(8,128)(2,1)}, u32[]{:S(2)}, u32[]{:S(2)}) %all-to-all-start.1) | async-done | bytes 5242912 | tf_op jit(solution)/shard_map/all_to_all | solution.py:90
  492.8 15.8 %gather_fusion.1 = bf16[1536,2048]{1,0:T(8,128)(2,1)} fusion(bf16[1280,2048]{1,0:T(8,128)(2,1)} %bitcast.11, s32[2048]{0:T(1024)S(1)} %pad_clamp_fusion.1), kind=kCustom, calls=%fused_computation.1 | custom fusion | bytes 12589056 | tf_op jit(solution)/shard_map/gather | solution.py:97
  508.7 10.9 %reshape.234 = bf16[256,6,2048]{2,1,0:T(8,128)(2,1)} reshape(bf16[1536,2048]{1,0:T(8,128)(2,1)} %gather_fusion.1) | data formatting | bytes 12582912 | tf_op jit(solution)/shard_map/gather | solution.py:97
  519.6 7.1 %fusion.78 = f32[256,1,2048]{2,1,0:T(1,128)} fusion(bf16[256,6,2048]{2,1,0:T(8,128)(2,1)} %reshape.234, bf16[256,6,1]{1,2,0:T(2,128)(2,1)S(1)} %copy.50), kind=kOutput, calls=%fused_computation.124 | convolution fusion | flops 6291456 | bytes 8391680 | tf_op jit(solution)/shard_map/tkd,tk->td/dot_general | solution.py:98
  526.7 5.9 fusion.6
  532.6 0.8 dynamic_slice.12
  533.4 51.3 %reduce-scatter.2.cloned.1.call-done = bf16[256,256]{1,0:T(8,128)(2,1)} async-done(((bf16[256,2048]{1,0:T(8,128)(2,1)}), bf16[256,256]{1,0:T(8,128)(2,1)}) %reduce-scatter.2.cloned.1.call-update) | async-done | bytes 131088 | tf_op jit(solution)/shard_map/reduce_scatter | solution.py:107
  584.7 1.0 fusion.47
  585.7 10.7 %all-gather.1 = f32[8,1,256]{2,1,0:T(1,128)S(1)} all-gather(f32[1,1,256]{2,1,0:T(1,128)S(1)} %bitcast.88), channel_id=2, replica_groups=mesh['ep'=32,'tp'=8] {'tp'}, dimensions={0}, use_global_device_ids=true | all-gather | bytes 9216 | tf_op jit(solution)/shard_map/all_gather | solution.py:113
  596.5 0.8 fusion.49
  (52 shorter events, 3.0 us)
Async XLA Ops:
  7.2 348.5 %copy-start = (bf16[1,352,2048]{2,1,0:T(8,128)(2,1)S(1)}, bf16[1,352,2048]{2,1,0:T(8,128)(2,1)}, u32[]{:S(2)}) copy-start(bf16[1,352,2048]{2,1,0:T(8,128)(2,1)} %param.18) | copy-start | bytes 4325380
  7.2 3.2 copy-start.4
  7.2 76.2 %all-reduce.2.cloned.1.call-start = ((), (), s32[]{:S(2)}) async-start(), calls=%async_computation.3 | async-start | bytes 4194304 | tf_op jit(solution)/shard_map/psum | solution.py:50
  83.4 2.3 copy-start.5
  106.9 241.7 %all-to-all-start = ((bf16[32,2,40,2048]{3,2,1,0:T(8,128)(2,1)}), bf16[32,2,40,2048]{3,2,1,0:T(8,128)(2,1)}, u32[]{:S(2)}, u32[]{:S(2)}) async-start(bf16[32,2,40,2048]{3,2,1,0:T(8,128)(2,1)} %broadcast_select_fusion), calls=%async_computation | async-start | bytes 20971520 | tf_op jit(solution)/shard_map/all_to_all | solution.py:75
  365.5 11.1 %copy-start.3 = (bf16[2048,64]{0,1:T(8,128)(2,1)S(1)}, bf16[2048,64]{0,1:T(8,128)(2,1)}, u32[]{:S(2)}) copy-start(bf16[2048,64]{0,1:T(8,128)(2,1)} %param.16) | copy-start | bytes 786436
  365.5 127.3 %all-to-all-start.1 = ((bf16[32,40,2048]{2,1,0:T(8,128)(2,1)}), bf16[32,40,2048]{2,1,0:T(8,128)(2,1)}, u32[]{:S(2)}, u32[]{:S(2)}) async-start(bf16[32,40,2048]{2,1,0:T(8,128)(2,1)} %convolution_convert_fusion), calls=%async_computation.1 | async-start | bytes 10485760 | tf_op jit(solution)/shard_map/all_to_all | solution.py:90
  375.7 209.0 %reduce-scatter.2.cloned.1.call-start = ((), (), s32[]{:S(2)}) async-start(), calls=%async_computation.4 | async-start | bytes 1179648 | tf_op jit(solution)/shard_map/reduce_scatter | solution.py:107
  526.7 70.6 %copy-start.1 = (bf16[1,352,2048]{2,1,0:T(8,128)(2,1)S(1)}, bf16[1,352,2048]{2,1,0:T(8,128)(2,1)}, u32[]{:S(2)}) copy-start(bf16[1,352,2048]{2,1,0:T(8,128)(2,1)} %param.18) | copy-start | bytes 4325380
  585.7 11.6 %copy-start.2 = (bf16[256,256]{1,0:T(8,128)(2,1)}, bf16[256,256]{1,0:T(8,128)(2,1)S(1)}, u32[]{:S(2)}) copy-start(bf16[256,256]{1,0:T(8,128)(2,1)S(1)} %get-tuple-element.3) | copy-start | bytes 393220
Sparse Core Ops, SparseCore 0:
  10.5 72.8 all-reduce.1
  532.7 51.9 reduce-scatter.1
